TPU v7x, 32 devices: a whole 2x2x4 slice. The times are simulated.
32 devices in a mesh: dp: 4 (over y, x), ctx: 8 (over z, core).
Axes of the slice: x: 2, y: 2, z: 4, core: 2. Of those that a mesh axis runs over, the one named last changes fastest.
Arguments:
- inputs: bfloat16 [4, 1024, 4096], P('dp', 'ctx'), may hold values from -8 to 8
- queries: bfloat16 [4, 1024, 8192], P('dp', 'ctx'), may hold values from -256 to 256
- grad_output: bfloat16 [4, 1024, 8192], P('dp', 'ctx'), may hold values from -6 to 6
- kv_weight: bfloat16 [4096, 1024], P(('dp', 'ctx')), may hold values from -1 to 1
Outputs:
- attn_out: bfloat16 [4, 1024, 8192], P('dp', 'ctx')
- grad_query: bfloat16 [4, 1024, 8192], P('dp', 'ctx')
- grad_inputs: bfloat16 [4, 1024, 4096], P('dp', 'ctx')
- grad_weight: float32 [4096, 1024], P(('dp', 'ctx'))
All inputs are finite; a program needn't handle non-finite values.
Results may differ from a plain program's by a relative error of at most 0.035.
Values may be sent and summed in bfloat16 or wider, within the bound.
No kernel may reach another device: no remote copies, remote signals or barrier semaphores. Data moves between devices by JAX's collectives and lax.ppermute only.
A program may use at most 128 MiB of HBM per device.

v0:
```python
import jax
import jax.numpy as jnp
from jax import lax
from jax.sharding import PartitionSpec as P

DH = 128
ROPE_BASE = 500000.0


def shifted(block, axis, distance):
    devices = range(lax.axis_size(axis))
    route = [(i - distance, i) for i in devices if i - distance in devices]
    return lax.ppermute(block, axis, route)


def shifted_2(value, axis, steps):
    count = lax.axis_size(axis)
    pairs = [(source, (source + steps) % count) for source in range(count)]
    return lax.ppermute(value, axis, pairs)


def rope_tables(positions, head_dim):
    half_dim = head_dim // 2
    frequency = ROPE_BASE ** (-2.0 * jnp.arange(half_dim, dtype=jnp.float32) / head_dim)
    angles = positions.astype(jnp.float32)[:, None] * frequency[None, :]
    return (jnp.cos(angles)[:, None, :], jnp.sin(angles)[:, None, :])


def rotary(values, positions):
    half_dim = values.shape[-1] // 2
    cosine, sine_table = rope_tables(positions, values.shape[-1])
    first_half = values[..., :half_dim]
    second = values[..., half_dim:]
    return jnp.concatenate(
        [first_half * cosine - second * sine_table, second * cosine + first_half * sine_table],
        axis=-1,
    )


def rotary_back(gradient, positions):
    half_dim = gradient.shape[-1] // 2
    cosine, sine_table = rope_tables(positions, gradient.shape[-1])
    first_half = gradient[..., :half_dim]
    second = gradient[..., half_dim:]
    return jnp.concatenate(
        [first_half * cosine + second * sine_table, second * cosine - first_half * sine_table],
        axis=-1,
    )


def on_device(inputs, queries, grad_output, kv_weight):
    token_count = inputs.shape[1]
    model_width = inputs.shape[2]
    kv_width = kv_weight.shape[1]
    kv_half = kv_width // 2
    head_dim = DH
    kv_heads = kv_half // head_dim
    q_heads = queries.shape[2] // head_dim
    group_size = q_heads // kv_heads
    row_count = group_size * token_count
    ctx_size = lax.axis_size("ctx")
    data_size = lax.axis_size("dp")
    ctx_index = lax.axis_index("ctx")
    score_scale = head_dim ** (-0.5)
    shard_rows = model_width // (data_size * ctx_size)
    tokens = inputs[0]
    weight_all = lax.all_gather(kv_weight, ("dp", "ctx"), axis=0, tiled=True)
    projected = jnp.dot(tokens, weight_all, preferred_element_type=jnp.float32)
    positions = ctx_index * token_count + jnp.arange(token_count, dtype=jnp.int32)
    key_rows = rotary(
        projected[:, :kv_half].reshape(token_count, kv_heads, head_dim), positions
    ).astype(jnp.bfloat16)
    value_rows = projected[:, kv_half:].astype(jnp.bfloat16)
    own_block = jnp.concatenate([key_rows.reshape(token_count, kv_half), value_rows], axis=1)

    def head_rows(matrix):
        return (
            matrix.reshape(token_count, kv_heads, group_size, head_dim)
            .transpose(1, 2, 0, 3)
            .reshape(kv_heads, row_count, head_dim)
        )

    def token_rows(rows_by_head):
        return (
            rows_by_head.reshape(kv_heads, group_size, token_count, head_dim)
            .transpose(2, 0, 1, 3)
            .reshape(token_count, q_heads * head_dim)
        )

    query_rows = head_rows(queries[0])
    grad_rows = head_rows(grad_output[0])
    query_pos = jnp.arange(row_count, dtype=jnp.int32) % token_count
    key_pos = jnp.arange(token_count, dtype=jnp.int32)

    def split_block(kv_block):
        key_part = kv_block[:, :kv_half].reshape(token_count, kv_heads, head_dim)
        value_part = kv_block[:, kv_half:].reshape(token_count, kv_heads, head_dim)
        return (key_part, value_part)

    def block_scores(key_part, block_id):
        scores = (
            jnp.einsum("hrd,khd->hrk", query_rows, key_part, preferred_element_type=jnp.float32)
            * score_scale
        )
        allowed = (block_id < ctx_index) | (query_pos[:, None] >= key_pos[None, :])
        return (scores, allowed)

    def forward_update(state_now, kv_block, block_id):
        row_top, row_total, row_accum = state_now
        key_part, value_part = split_block(kv_block)
        scores, allowed = block_scores(key_part, block_id)
        scores = jnp.where(allowed[None], scores, -jnp.inf)
        new_top = jnp.maximum(row_top, jnp.max(scores, axis=-1, keepdims=True))
        weights = jnp.exp(scores - new_top)
        factor = jnp.exp(row_top - new_top)
        row_total = row_total * factor + jnp.sum(weights, axis=-1, keepdims=True)
        row_accum = row_accum * factor + jnp.einsum(
            "hrk,khd->hrd",
            weights.astype(jnp.bfloat16),
            value_part,
            preferred_element_type=jnp.float32,
        )
        return (new_top, row_total, row_accum)

    start_state = (
        jnp.full((kv_heads, row_count, 1), -jnp.inf, jnp.float32),
        jnp.zeros((kv_heads, row_count, 1), jnp.float32),
        jnp.zeros((kv_heads, row_count, head_dim), jnp.float32),
    )
    state_now = forward_update(start_state, own_block, ctx_index)
    kv_store = jnp.zeros((ctx_size, token_count, kv_width), jnp.bfloat16)
    kv_store = lax.dynamic_update_slice_in_dim(kv_store, own_block[None], ctx_index, 0)

    def forward_step(offset, loop_state):
        kv_block, stored_now, state_here = loop_state
        kv_block = shifted(kv_block, "ctx", 1)
        source = ctx_index - offset

        def take_block(operands):
            stored, current = operands
            stored = lax.dynamic_update_slice_in_dim(stored, kv_block[None], source, 0)
            return (stored, forward_update(current, kv_block, source))

        def keep_state(operands):
            return operands

        stored_now, state_here = lax.cond(
            offset <= ctx_index, take_block, keep_state, (stored_now, state_here)
        )
        return (kv_block, stored_now, state_here)

    last_block, kv_store, state_now = lax.fori_loop(
        1, ctx_size, forward_step, (own_block, kv_store, state_now)
    )
    row_top, row_total, row_accum = state_now
    attn_rows = (row_accum / row_total).astype(jnp.bfloat16)
    log_total = row_top + jnp.log(row_total)
    row_delta = jnp.sum(
        grad_rows.astype(jnp.float32) * attn_rows.astype(jnp.float32), axis=-1, keepdims=True
    )
    attn_out = token_rows(attn_rows)[None]

    def backward_terms(kv_block, block_id):
        key_part, value_part = split_block(kv_block)
        scores, allowed = block_scores(key_part, block_id)
        probs_now = jnp.where(allowed[None], jnp.exp(scores - log_total), 0.0)
        dprobs = jnp.einsum(
            "hrd,khd->hrk", grad_rows, value_part, preferred_element_type=jnp.float32
        )
        dscores = (probs_now * (dprobs - row_delta)).astype(jnp.bfloat16)
        grad_keys = (
            jnp.einsum("hrk,hrd->khd", dscores, query_rows, preferred_element_type=jnp.float32)
            * score_scale
        )
        grad_values = jnp.einsum(
            "hrk,hrd->khd",
            probs_now.astype(jnp.bfloat16),
            grad_rows,
            preferred_element_type=jnp.float32,
        )
        query_part = jnp.einsum(
            "hrk,khd->hrd", dscores, key_part, preferred_element_type=jnp.float32
        )
        block_grads = jnp.concatenate(
            [grad_keys.reshape(token_count, kv_half), grad_values.reshape(token_count, kv_half)],
            axis=1,
        )
        return (block_grads, query_part)

    def add_block(operands, block_id):
        grad_block, grad_query_sum = operands
        kv_block = lax.dynamic_slice_in_dim(kv_store, block_id, 1, 0)[0]
        block_grads, query_part = backward_terms(kv_block, block_id)
        return (grad_block + block_grads, grad_query_sum + query_part)

    def skip_block(operand_pair):
        return operand_pair

    zero_grads = jnp.zeros((token_count, kv_width), jnp.float32)
    zero_query = jnp.zeros((kv_heads, row_count, head_dim), jnp.float32)

    def backward_step(offset, operands):
        source = ctx_index - offset

        def include(operand_pair):
            return add_block(operand_pair, source)

        grad_block, grad_query_sum = lax.cond(offset <= ctx_index, include, skip_block, operands)
        grad_block = shifted_2(grad_block.astype(jnp.bfloat16), "ctx", 1).astype(grad_block.dtype)
        return (grad_block, grad_query_sum)

    grad_block, grad_query_sum = lax.fori_loop(0, ctx_size, backward_step, (zero_grads, zero_query))
    grad_query = token_rows(grad_query_sum * score_scale).astype(jnp.bfloat16)[None]
    grad_key_rows = rotary_back(
        grad_block[:, :kv_half].reshape(token_count, kv_heads, head_dim), positions
    ).reshape(token_count, kv_half)
    grad_projected = jnp.concatenate([grad_key_rows, grad_block[:, kv_half:]], axis=1).astype(
        jnp.bfloat16
    )
    grad_inputs = lax.dot_general(
        grad_projected, weight_all, (((1,), (1,)), ((), ())), preferred_element_type=jnp.float32
    ).astype(jnp.bfloat16)[None]
    reordered = (
        tokens.reshape(token_count, data_size, ctx_size, shard_rows)
        .transpose(0, 2, 1, 3)
        .reshape(token_count, model_width)
    )
    partial_sum = lax.psum_scatter(
        lax.dot_general(
            reordered, grad_projected, (((0,), (0,)), ((), ())), preferred_element_type=jnp.float32
        ).astype(jnp.bfloat16),
        "ctx",
        scatter_dimension=0,
        tiled=True,
    )
    grad_weight = lax.psum_scatter(partial_sum, "dp", scatter_dimension=0, tiled=True).astype(
        jnp.float32
    )
    return (attn_out, grad_query, grad_inputs, grad_weight)


def solution(mesh):
    in_specs = (
        P("dp", "ctx", None),
        P("dp", "ctx", None),
        P("dp", "ctx", None),
        P(("dp", "ctx"), None),
    )
    out_specs = (
        P("dp", "ctx", None),
        P("dp", "ctx", None),
        P("dp", "ctx", None),
        P(("dp", "ctx"), None),
    )
    return jax.shard_map(
        on_device, mesh=mesh, in_specs=in_specs, out_specs=out_specs, check_vma=False
    )
```

profile of v0, /device:TPU:0, one launch (start us, length us, event | category | flops | bytes accessed | tf_op | source)
XLA Modules:
  0.0 496.9 jit_solution(8035987753920673615)
XLA Ops:
  8.0 3.5 copy.141
  11.5 4.3 copy.110
  15.8 2.3 reshape.240
  18.1 2.2 copy.139
  20.2 3.8 copy.102
  24.1 2.8 reshape.237
  26.9 2.5 copy.107
  29.4 2.3 copy.115
  31.6 2.3 copy.116
  35.2 55.6 %all-gather.2.cloned.1.call-done = bf16[4096,1024]{1,0:T(8,128)(2,1)} async-done(((bf16[128,1024]{1,0:T(8,128)(2,1)}), bf16[4096,1024]{1,0:T(8,128)(2,1)}) %all-gather.2.cloned.1.call-update) | async-done | bytes 8388624 | tf_op jit(solution)/shard_map/all_gather | solution.py:67
  90.8 5.0 fusion.27
  102.1 1.8 copy.101
  103.9 2.1 fusion.41
  106.7 3.3 convolution_add_fusion.1
  111.7 71.5 %while.38 = (s32[]{:T(128)}, bf16[128,1024]{0,1:T(8,128)(2,1)S(1)}, bf16[8,128,1024]{1,2,0:T(8,128)(2,1)}, f32[4,2048,1]{1,0,2:T(4,128)S(1)}, f32[4,2048,1]{1,0,...) while((s32[]{:T(128)}, bf16[128,1024]{0,1:T(8,128)(2,1)S(1)}, ...), condition=%wide.region_7.8_spmd.clone, body=%wide.region_2.7_spmd.clone.sunk | while | flops 551063552 | bytes 61154760 | solution.py:152
  111.7 2.2 collective-permute-start
  115.0 15.1 %collective-permute-start = (bf16[128,1024]{0,1:T(8,128)(2,1)S(1)}, bf16[128,1024]{0,1:T(8,128)(2,1)S(1)}, u32[]{:S(2)}, u32[]{:S(2)}) collective-permute-start(bf16[128,1024]{0,1:T(8,128)(2,1)S(1)} %get-tuple-element.850), channel_id=1, source_target_pairs={{0,1},{1,2},{2,3},{3,4},{4,5},{5,6},{6,7},{8,9},{9,10},{10,11},{11... | collective-permute-start | bytes 786440 | tf_op jit(solution)/shard_map/while/body/eval_jaxpr/ppermute | solution.py:13
  131.3 6.6 %collective-permute-start = (bf16[128,1024]{0,1:T(8,128)(2,1)S(1)}, bf16[128,1024]{0,1:T(8,128)(2,1)S(1)}, u32[]{:S(2)}, u32[]{:S(2)}) collective-permute-start(bf16[128,1024]{0,1:T(8,128)(2,1)S(1)} %get-tuple-element.850), channel_id=1, source_target_pairs={{0,1},{1,2},{2,3},{3,4},{4,5},{5,6},{6,7},{8,9},{9,10},{10,11},{11... | collective-permute-start | bytes 786440 | tf_op jit(solution)/shard_map/while/body/eval_jaxpr/ppermute | solution.py:13
  139.0 16.2 %collective-permute-start = (bf16[128,1024]{0,1:T(8,128)(2,1)S(1)}, bf16[128,1024]{0,1:T(8,128)(2,1)S(1)}, u32[]{:S(2)}, u32[]{:S(2)}) collective-permute-start(bf16[128,1024]{0,1:T(8,128)(2,1)S(1)} %get-tuple-element.850), channel_id=1, source_target_pairs={{0,1},{1,2},{2,3},{3,4},{4,5},{5,6},{6,7},{8,9},{9,10},{10,11},{11... | collective-permute-start | bytes 786440 | tf_op jit(solution)/shard_map/while/body/eval_jaxpr/ppermute | solution.py:13
  156.4 6.6 %collective-permute-start = (bf16[128,1024]{0,1:T(8,128)(2,1)S(1)}, bf16[128,1024]{0,1:T(8,128)(2,1)S(1)}, u32[]{:S(2)}, u32[]{:S(2)}) collective-permute-start(bf16[128,1024]{0,1:T(8,128)(2,1)S(1)} %get-tuple-element.850), channel_id=1, source_target_pairs={{0,1},{1,2},{2,3},{3,4},{4,5},{5,6},{6,7},{8,9},{9,10},{10,11},{11... | collective-permute-start | bytes 786440 | tf_op jit(solution)/shard_map/while/body/eval_jaxpr/ppermute | solution.py:13
  164.2 10.2 %collective-permute-start = (bf16[128,1024]{0,1:T(8,128)(2,1)S(1)}, bf16[128,1024]{0,1:T(8,128)(2,1)S(1)}, u32[]{:S(2)}, u32[]{:S(2)}) collective-permute-start(bf16[128,1024]{0,1:T(8,128)(2,1)S(1)} %get-tuple-element.850), channel_id=1, source_target_pairs={{0,1},{1,2},{2,3},{3,4},{4,5},{5,6},{6,7},{8,9},{9,10},{10,11},{11... | collective-permute-start | bytes 786440 | tf_op jit(solution)/shard_map/while/body/eval_jaxpr/ppermute | solution.py:13
  175.5 6.6 %collective-permute-start = (bf16[128,1024]{0,1:T(8,128)(2,1)S(1)}, bf16[128,1024]{0,1:T(8,128)(2,1)S(1)}, u32[]{:S(2)}, u32[]{:S(2)}) collective-permute-start(bf16[128,1024]{0,1:T(8,128)(2,1)S(1)} %get-tuple-element.850), channel_id=1, source_target_pairs={{0,1},{1,2},{2,3},{3,4},{4,5},{5,6},{6,7},{8,9},{9,10},{10,11},{11... | collective-permute-start | bytes 786440 | tf_op jit(solution)/shard_map/while/body/eval_jaxpr/ppermute | solution.py:13
  183.2 5.4 %copy.108 = f32[4,2048,128]{1,2,0:T(8,128)} copy(f32[4,2048,128]{2,1,0:T(8,128)} %get-tuple-element.456) | data formatting | bytes 8388608 | tf_op jit(solution)/shard_map/while | solution.py:152
  188.7 5.0 %multiply_reduce_fusion = (f32[4,2048]{1,0:T(4,128)S(1)}, bf16[4,2048,128]{1,2,0:T(8,128)(2,1)}) fusion(bf16[4,2048,128]{1,2,0:T(8,128)(2,1)} %reshape.240, f32[4,2048,128]{1,2,0:T(8,128)} %copy.108, f32[4,2048]{1,0:T(4,128)S(1)} %bitcast.152), kind=kLoop, calls=%fused_computation.44 | loop fusion | flops 6283264 | bytes 8454144 | tf_op jit(solution)/shard_map/reduce_sum | solution.py:158
  193.7 2.2 broadcast.182
  195.9 169.3 %while.39 = (s32[]{:T(128)}, f32[128,1024]{0,1:T(8,128)S(1)}, f32[4,2048,128]{2,1,0:T(8,128)}, s32[]{:T(128)}, bf16[8,128,1024]{1,2,0:T(8,128)(2,1)}, /*index=5*...) while((s32[]{:T(128)}, f32[128,1024]{0,1:T(8,128)S(1)}, ...), condition=%wide.region_12.13_spmd.clone, body=%wide.region_9.12_spmd.clone.sunk | while | flops 1351823360 | bytes 85468640 | solution.py:212
  196.0 10.5 %conditional.7 = ((f32[128,1024]{0,1:T(8,128)S(1)}, f32[4,2048,128]{2,1,0:T(8,128)})) conditional(s32[]{:T(128)} %convert_element_type.142, (f32[128,1024]{0,1:T(8,128)S(1)}, f32[4,2048,128]{2,1,0:T(8,128)}) %tuple.112, (s32[]{:T(128)}, s32[]{:T(128)}, s32[2048]{0:T(1024)S(1)}, s32[128]{0:T(128)S(1)}, bf16[8,128,1024]{1,2,0:T(8,128)(2,1)}, ...), branch_computations={%region_10.10_spmd, %region_11.11_spmd.clone} | conditional | flops 1351428096 | bytes 81781416 | solution.py:208
  202.4 2.2 convolution_add_fusion
  204.6 1.9 copy-done.4
  206.5 14.3 %collective-permute-start.1 = (bf16[128,1024]{0,1:T(8,128)(2,1)S(1)}, bf16[128,1024]{0,1:T(8,128)(2,1)S(1)}, u32[]{:S(2)}, u32[]{:S(2)}) collective-permute-start(bf16[128,1024]{0,1:T(8,128)(2,1)S(1)} %convert_element_type.143), channel_id=1, source_target_pairs={{0,1},{1,2},{2,3},{3,4},{4,5},{5,6},{6,7},{7,0},{8,9},{9,10},{10,1... | collective-permute-start | bytes 786440 | tf_op jit(solution)/shard_map/while/body/eval_jaxpr/ppermute | solution.py:19
  220.9 37.2 %collective-permute-done.1 = bf16[128,1024]{0,1:T(8,128)(2,1)S(1)} collective-permute-done((bf16[128,1024]{0,1:T(8,128)(2,1)S(1)}, bf16[128,1024]{0,1:T(8,128)(2,1)S(1)}, u32[]{:S(2)}, u32[]{:S(2)}) %collective-permute-start.1) | collective-permute-done | bytes 262176 | tf_op jit(solution)/shard_map/while/body/eval_jaxpr/ppermute | solution.py:19
  258.3 13.8 %collective-permute-done.1 = bf16[128,1024]{0,1:T(8,128)(2,1)S(1)} collective-permute-done((bf16[128,1024]{0,1:T(8,128)(2,1)S(1)}, bf16[128,1024]{0,1:T(8,128)(2,1)S(1)}, u32[]{:S(2)}, u32[]{:S(2)}) %collective-permute-start.1) | collective-permute-done | bytes 262176 | tf_op jit(solution)/shard_map/while/body/eval_jaxpr/ppermute | solution.py:19
  272.4 13.8 %collective-permute-done.1 = bf16[128,1024]{0,1:T(8,128)(2,1)S(1)} collective-permute-done((bf16[128,1024]{0,1:T(8,128)(2,1)S(1)}, bf16[128,1024]{0,1:T(8,128)(2,1)S(1)}, u32[]{:S(2)}, u32[]{:S(2)}) %collective-permute-start.1) | collective-permute-done | bytes 262176 | tf_op jit(solution)/shard_map/while/body/eval_jaxpr/ppermute | solution.py:19
  286.5 13.8 %collective-permute-done.1 = bf16[128,1024]{0,1:T(8,128)(2,1)S(1)} collective-permute-done((bf16[128,1024]{0,1:T(8,128)(2,1)S(1)}, bf16[128,1024]{0,1:T(8,128)(2,1)S(1)}, u32[]{:S(2)}, u32[]{:S(2)}) %collective-permute-start.1) | collective-permute-done | bytes 262176 | tf_op jit(solution)/shard_map/while/body/eval_jaxpr/ppermute | solution.py:19
  300.6 14.8 %collective-permute-done.1 = bf16[128,1024]{0,1:T(8,128)(2,1)S(1)} collective-permute-done((bf16[128,1024]{0,1:T(8,128)(2,1)S(1)}, bf16[128,1024]{0,1:T(8,128)(2,1)S(1)}, u32[]{:S(2)}, u32[]{:S(2)}) %collective-permute-start.1) | collective-permute-done | bytes 262176 | tf_op jit(solution)/shard_map/while/body/eval_jaxpr/ppermute | solution.py:19
  315.7 16.3 %collective-permute-done.1 = bf16[128,1024]{0,1:T(8,128)(2,1)S(1)} collective-permute-done((bf16[128,1024]{0,1:T(8,128)(2,1)S(1)}, bf16[128,1024]{0,1:T(8,128)(2,1)S(1)}, u32[]{:S(2)}, u32[]{:S(2)}) %collective-permute-start.1) | collective-permute-done | bytes 262176 | tf_op jit(solution)/shard_map/while/body/eval_jaxpr/ppermute | solution.py:19
  332.3 16.3 %collective-permute-done.1 = bf16[128,1024]{0,1:T(8,128)(2,1)S(1)} collective-permute-done((bf16[128,1024]{0,1:T(8,128)(2,1)S(1)}, bf16[128,1024]{0,1:T(8,128)(2,1)S(1)}, u32[]{:S(2)}, u32[]{:S(2)}) %collective-permute-start.1) | collective-permute-done | bytes 262176 | tf_op jit(solution)/shard_map/while/body/eval_jaxpr/ppermute | solution.py:19
  348.9 16.3 %collective-permute-done.1 = bf16[128,1024]{0,1:T(8,128)(2,1)S(1)} collective-permute-done((bf16[128,1024]{0,1:T(8,128)(2,1)S(1)}, bf16[128,1024]{0,1:T(8,128)(2,1)S(1)}, u32[]{:S(2)}, u32[]{:S(2)}) %collective-permute-start.1) | collective-permute-done | bytes 262176 | tf_op jit(solution)/shard_map/while/body/eval_jaxpr/ppermute | solution.py:19
  366.4 5.6 %convert_bitcast_fusion = bf16[4096,1024]{0,1:T(8,128)(2,1)} fusion(bf16[128,4096]{0,1:T(8,128)(2,1)S(1)} %bitcast.151, bf16[128,512]{0,1:T(8,128)(2,1)S(1)} %slice.61, bf16[128,512]{0,1:T(8,128)(2,1)S(1)} %bitcast.158), kind=kOutput, calls=%fused_computation.39 | convolution fusion | flops 1078460416 | bytes 9699328 | tf_op jit(solution)/shard_map/dot_general | solution.py:229
  372.1 86.9 %reduce-scatter.5.cloned.1.call-done = bf16[512,1024]{0,1:T(8,128)(2,1)} async-done(((bf16[4096,1024]{0,1:T(8,128)(2,1)}), bf16[512,1024]{0,1:T(8,128)(2,1)}) %reduce-scatter.5.cloned.1.call-update) | async-done | bytes 1048592 | tf_op jit(solution)/shard_map/reduce_scatter | solution.py:228
  458.9 2.3 copy.131
  461.3 2.2 copy.140
  463.5 3.8 copy.109
  467.2 4.2 broadcast_in_dim_reshape.3
  471.4 2.8 multiply_convert_fusion
  475.6 2.3 convert_element_type.107
  477.9 7.3 %fusion.22 = bf16[1,128,4096]{2,1,0:T(8,128)(2,1)} fusion(bf16[4096,1024]{1,0:T(8,128)(2,1)} %all-gather.2.cloned.1.call-done, bf16[128,512]{0,1:T(8,128)(2,1)S(1)} %slice.61, bf16[128,512]{0,1:T(8,128)(2,1)S(1)} %bitcast.159), kind=kOutput, calls=%fused_computation.41 | convolution fusion | flops 1074790400 | bytes 9699328 | tf_op jit(solution)/shard_map/dot_general | solution.py:220
  485.1 3.2 reduce-scatter.7.cloned.1.call-done
  (171 shorter events, 30.9 us)
Async XLA Ops:
  7.2 83.6 %all-gather.2.cloned.1.call-start = ((), (), s32[]{:S(2)}) async-start(), calls=%async_computation.2 | async-start | bytes 8650752 | tf_op jit(solution)/shard_map/all_gather | solution.py:67
  7.9 451.1 %reduce-scatter.5.cloned.1.call-start = ((), (), s32[]{:S(2)}) async-start(), calls=%async_computation.3 | async-start | bytes 9437184 | tf_op jit(solution)/shard_map/reduce_scatter | solution.py:228
  34.3 64.1 %copy-start.8 = (f32[128,64]{1,0:T(8,128)}, f32[128,64]{1,0:T(8,128)S(1)}, u32[]{:S(2)}) copy-start(f32[128,64]{1,0:T(8,128)S(1)} %get-tuple-element.707) | copy-start | bytes 98308
  34.3 64.1 %copy-start.10 = (f32[128,64]{1,0:T(8,128)}, f32[128,64]{1,0:T(8,128)S(1)}, u32[]{:S(2)}) copy-start(f32[128,64]{1,0:T(8,128)S(1)} %get-tuple-element.708) | copy-start | bytes 98308
  106.7 3.6 copy-start.7
  106.7 5.0 copy-start.12
  110.4 1.3 copy-start.5
  111.7 3.3 collective-permute-start
  115.0 16.2 %collective-permute-start = (bf16[128,1024]{0,1:T(8,128)(2,1)S(1)}, bf16[128,1024]{0,1:T(8,128)(2,1)S(1)}, u32[]{:S(2)}, u32[]{:S(2)}) collective-permute-start(bf16[128,1024]{0,1:T(8,128)(2,1)S(1)} %get-tuple-element.850), channel_id=1, source_target_pairs={{0,1},{1,2},{2,3},{3,4},{4,5},{5,6},{6,7},{8,9},{9,10},{10,11},{11... | collective-permute-start | bytes 786440 | tf_op jit(solution)/shard_map/while/body/eval_jaxpr/ppermute | solution.py:13
  131.3 7.7 %collective-permute-start = (bf16[128,1024]{0,1:T(8,128)(2,1)S(1)}, bf16[128,1024]{0,1:T(8,128)(2,1)S(1)}, u32[]{:S(2)}, u32[]{:S(2)}) collective-permute-start(bf16[128,1024]{0,1:T(8,128)(2,1)S(1)} %get-tuple-element.850), channel_id=1, source_target_pairs={{0,1},{1,2},{2,3},{3,4},{4,5},{5,6},{6,7},{8,9},{9,10},{10,11},{11... | collective-permute-start | bytes 786440 | tf_op jit(solution)/shard_map/while/body/eval_jaxpr/ppermute | solution.py:13
  139.0 17.3 %collective-permute-start = (bf16[128,1024]{0,1:T(8,128)(2,1)S(1)}, bf16[128,1024]{0,1:T(8,128)(2,1)S(1)}, u32[]{:S(2)}, u32[]{:S(2)}) collective-permute-start(bf16[128,1024]{0,1:T(8,128)(2,1)S(1)} %get-tuple-element.850), channel_id=1, source_target_pairs={{0,1},{1,2},{2,3},{3,4},{4,5},{5,6},{6,7},{8,9},{9,10},{10,11},{11... | collective-permute-start | bytes 786440 | tf_op jit(solution)/shard_map/while/body/eval_jaxpr/ppermute | solution.py:13
  156.4 7.7 %collective-permute-start = (bf16[128,1024]{0,1:T(8,128)(2,1)S(1)}, bf16[128,1024]{0,1:T(8,128)(2,1)S(1)}, u32[]{:S(2)}, u32[]{:S(2)}) collective-permute-start(bf16[128,1024]{0,1:T(8,128)(2,1)S(1)} %get-tuple-element.850), channel_id=1, source_target_pairs={{0,1},{1,2},{2,3},{3,4},{4,5},{5,6},{6,7},{8,9},{9,10},{10,11},{11... | collective-permute-start | bytes 786440 | tf_op jit(solution)/shard_map/while/body/eval_jaxpr/ppermute | solution.py:13
  164.2 11.3 %collective-permute-start = (bf16[128,1024]{0,1:T(8,128)(2,1)S(1)}, bf16[128,1024]{0,1:T(8,128)(2,1)S(1)}, u32[]{:S(2)}, u32[]{:S(2)}) collective-permute-start(bf16[128,1024]{0,1:T(8,128)(2,1)S(1)} %get-tuple-element.850), channel_id=1, source_target_pairs={{0,1},{1,2},{2,3},{3,4},{4,5},{5,6},{6,7},{8,9},{9,10},{10,11},{11... | collective-permute-start | bytes 786440 | tf_op jit(solution)/shard_map/while/body/eval_jaxpr/ppermute | solution.py:13
  175.5 7.7 %collective-permute-start = (bf16[128,1024]{0,1:T(8,128)(2,1)S(1)}, bf16[128,1024]{0,1:T(8,128)(2,1)S(1)}, u32[]{:S(2)}, u32[]{:S(2)}) collective-permute-start(bf16[128,1024]{0,1:T(8,128)(2,1)S(1)} %get-tuple-element.850), channel_id=1, source_target_pairs={{0,1},{1,2},{2,3},{3,4},{4,5},{5,6},{6,7},{8,9},{9,10},{10,11},{11... | collective-permute-start | bytes 786440 | tf_op jit(solution)/shard_map/while/body/eval_jaxpr/ppermute | solution.py:13
  195.9 169.7 %copy-start.9 = (f32[128,64]{1,0:T(8,128)S(1)}, f32[128,64]{1,0:T(8,128)}, u32[]{:S(2)}) copy-start(f32[128,64]{1,0:T(8,128)} %copy-done.8) | copy-start | bytes 98308
  195.9 169.7 %copy-start.11 = (f32[128,64]{1,0:T(8,128)S(1)}, f32[128,64]{1,0:T(8,128)}, u32[]{:S(2)}) copy-start(f32[128,64]{1,0:T(8,128)} %copy-done.10) | copy-start | bytes 98308
  197.0 1.7 copy-start
  200.2 2.2 copy-start.3
  204.6 1.9 copy-start.4
  206.5 51.5 %collective-permute-start.1 = (bf16[128,1024]{0,1:T(8,128)(2,1)S(1)}, bf16[128,1024]{0,1:T(8,128)(2,1)S(1)}, u32[]{:S(2)}, u32[]{:S(2)}) collective-permute-start(bf16[128,1024]{0,1:T(8,128)(2,1)S(1)} %convert_element_type.143), channel_id=1, source_target_pairs={{0,1},{1,2},{2,3},{3,4},{4,5},{5,6},{6,7},{7,0},{8,9},{9,10},{10,1... | collective-permute-start | bytes 786440 | tf_op jit(solution)/shard_map/while/body/eval_jaxpr/ppermute | solution.py:19
  258.3 13.9 %collective-permute-start.1 = (bf16[128,1024]{0,1:T(8,128)(2,1)S(1)}, bf16[128,1024]{0,1:T(8,128)(2,1)S(1)}, u32[]{:S(2)}, u32[]{:S(2)}) collective-permute-start(bf16[128,1024]{0,1:T(8,128)(2,1)S(1)} %convert_element_type.143), channel_id=1, source_target_pairs={{0,1},{1,2},{2,3},{3,4},{4,5},{5,6},{6,7},{7,0},{8,9},{9,10},{10,1... | collective-permute-start | bytes 786440 | tf_op jit(solution)/shard_map/while/body/eval_jaxpr/ppermute | solution.py:19
  272.4 13.9 %collective-permute-start.1 = (bf16[128,1024]{0,1:T(8,128)(2,1)S(1)}, bf16[128,1024]{0,1:T(8,128)(2,1)S(1)}, u32[]{:S(2)}, u32[]{:S(2)}) collective-permute-start(bf16[128,1024]{0,1:T(8,128)(2,1)S(1)} %convert_element_type.143), channel_id=1, source_target_pairs={{0,1},{1,2},{2,3},{3,4},{4,5},{5,6},{6,7},{7,0},{8,9},{9,10},{10,1... | collective-permute-start | bytes 786440 | tf_op jit(solution)/shard_map/while/body/eval_jaxpr/ppermute | solution.py:19
  286.5 13.9 %collective-permute-start.1 = (bf16[128,1024]{0,1:T(8,128)(2,1)S(1)}, bf16[128,1024]{0,1:T(8,128)(2,1)S(1)}, u32[]{:S(2)}, u32[]{:S(2)}) collective-permute-start(bf16[128,1024]{0,1:T(8,128)(2,1)S(1)} %convert_element_type.143), channel_id=1, source_target_pairs={{0,1},{1,2},{2,3},{3,4},{4,5},{5,6},{6,7},{7,0},{8,9},{9,10},{10,1... | collective-permute-start | bytes 786440 | tf_op jit(solution)/shard_map/while/body/eval_jaxpr/ppermute | solution.py:19
  300.5 14.9 %collective-permute-start.1 = (bf16[128,1024]{0,1:T(8,128)(2,1)S(1)}, bf16[128,1024]{0,1:T(8,128)(2,1)S(1)}, u32[]{:S(2)}, u32[]{:S(2)}) collective-permute-start(bf16[128,1024]{0,1:T(8,128)(2,1)S(1)} %convert_element_type.143), channel_id=1, source_target_pairs={{0,1},{1,2},{2,3},{3,4},{4,5},{5,6},{6,7},{7,0},{8,9},{9,10},{10,1... | collective-permute-start | bytes 786440 | tf_op jit(solution)/shard_map/while/body/eval_jaxpr/ppermute | solution.py:19
  315.7 16.4 %collective-permute-start.1 = (bf16[128,1024]{0,1:T(8,128)(2,1)S(1)}, bf16[128,1024]{0,1:T(8,128)(2,1)S(1)}, u32[]{:S(2)}, u32[]{:S(2)}) collective-permute-start(bf16[128,1024]{0,1:T(8,128)(2,1)S(1)} %convert_element_type.143), channel_id=1, source_target_pairs={{0,1},{1,2},{2,3},{3,4},{4,5},{5,6},{6,7},{7,0},{8,9},{9,10},{10,1... | collective-permute-start | bytes 786440 | tf_op jit(solution)/shard_map/while/body/eval_jaxpr/ppermute | solution.py:19
  332.2 16.4 %collective-permute-start.1 = (bf16[128,1024]{0,1:T(8,128)(2,1)S(1)}, bf16[128,1024]{0,1:T(8,128)(2,1)S(1)}, u32[]{:S(2)}, u32[]{:S(2)}) collective-permute-start(bf16[128,1024]{0,1:T(8,128)(2,1)S(1)} %convert_element_type.143), channel_id=1, source_target_pairs={{0,1},{1,2},{2,3},{3,4},{4,5},{5,6},{6,7},{7,0},{8,9},{9,10},{10,1... | collective-permute-start | bytes 786440 | tf_op jit(solution)/shard_map/while/body/eval_jaxpr/ppermute | solution.py:19
  348.8 16.4 %collective-permute-start.1 = (bf16[128,1024]{0,1:T(8,128)(2,1)S(1)}, bf16[128,1024]{0,1:T(8,128)(2,1)S(1)}, u32[]{:S(2)}, u32[]{:S(2)}) collective-permute-start(bf16[128,1024]{0,1:T(8,128)(2,1)S(1)} %convert_element_type.143), channel_id=1, source_target_pairs={{0,1},{1,2},{2,3},{3,4},{4,5},{5,6},{6,7},{7,0},{8,9},{9,10},{10,1... | collective-permute-start | bytes 786440 | tf_op jit(solution)/shard_map/while/body/eval_jaxpr/ppermute | solution.py:19
  365.2 1.2 copy-start.6
  372.0 116.3 %reduce-scatter.7.cloned.1.call-start = ((), (), s32[]{:S(2)}) async-start(), calls=%async_computation.4 | async-start | bytes 1310720
Sparse Core Ops, SparseCore 0:
  11.0 79.7 all-gather.1
  372.2 86.7 reduce-scatter.4
  461.8 26.4 reduce-scatter.6
where the time goes:
time: 498 us; the launch traced here: 497 us
  waiting for transfers between devices  297 us (60%)
  starting transfers between devices  78.1 us (16%)
  local copies, waits for them, and re-layouts  65 us (13%)
  matrix products  29 us (6%)
  between operations  14 us (3%)
  other arithmetic  13.1 us (3%)
    ppermute x8, waiting for transfers between devices, shifted_2(): return lax.ppermute(value, axis, pairs)  142 us
    reduce_scatter x1, waiting for transfers between devices, on_device(): lax.psum_scatter(lax.dot_general(reordered, grad_projected, (((0,), (0,))...  86.9 us
    ppermute x7, starting transfers between devices, shifted(): return lax.ppermute(block, axis, route)  63.3 us
    all_gather x1, waiting for transfers between devices, on_device(): weight_all = lax.all_gather(kv_weight, ('dp', 'ctx'), axis=0, tiled=True)  55.6 us
    unnamed x27, local copies, waits for them, and re-layouts  20.9 us
    ppermute x8, starting transfers between devices, shifted_2(): return lax.ppermute(value, axis, pairs)  14.7 us
  transfers between devices with their start and end apart: 18, of which 18 were waited for; matrix products, arithmetic and copies ran while one was open for 10% of the time, Pallas kernels for 0%

commit v1 on v0

--- a/solution.py
+++ b/solution.py
@@ -64,7 +64,10 @@
     score_scale = head_dim ** (-0.5)
     shard_rows = model_width // (data_size * ctx_size)
     tokens = inputs[0]
-    weight_all = lax.all_gather(kv_weight, ("dp", "ctx"), axis=0, tiled=True)
+    weight_all = jnp.concatenate(
+        lax.all_to_all(jnp.stack([kv_weight] * lax.axis_size(("dp", "ctx"))), ("dp", "ctx"), 0, 0),
+        axis=0,
+    )
     projected = jnp.dot(tokens, weight_all, preferred_element_type=jnp.float32)
     positions = ctx_index * token_count + jnp.arange(token_count, dtype=jnp.int32)
     key_rows = rotary(

time: 498 us -> 612 us (1.23)
  waiting for transfers between devices: 297 us -> 399 us
  local copies, waits for them, and re-layouts: 65 us -> 71.8 us
    all_to_all x0 -> x1, waiting for transfers between devices: none -> 159 us  [on_device(): lax.all_to_all(jnp.stack([kv_weight] * lax.axis_size(('dp', 'ctx'))), ('d...]
    all_gather x1 -> x0, waiting for transfers between devices: 55.6 us -> none  [on_device(): weight_all = lax.all_gather(kv_weight, ('dp', 'ctx'), axis=0, tiled=True)]
    all_to_all x0 -> x1, starting transfers between devices: none -> 7.45 us  [on_device(): lax.all_to_all(jnp.stack([kv_weight] * lax.axis_size(('dp', 'ctx'))), ('d...]
    unnamed x27 -> x29, local copies, waits for them, and re-layouts: 20.9 us -> 19.3 us
  transfers between devices with their start and end apart: 18 -> 18, of which waited for: 18 -> 17; matrix products, arithmetic and copies ran while one was open for 10% -> 9% of each run, Pallas kernels for 0% -> 0%
where the time goes in v1:
time: 612 us; the launch traced here: 610 us
  waiting for transfers between devices  399 us (65%)
  starting transfers between devices  82 us (13%)
  local copies, waits for them, and re-layouts  71.8 us (12%)
  matrix products  29.1 us (5%)
  between operations  14.4 us (2%)
  other arithmetic  13 us (2%)
    all_to_all x1, waiting for transfers between devices, on_device(): lax.all_to_all(jnp.stack([kv_weight] * lax.axis_size(('dp', 'ctx'))), ('d...  159 us
    ppermute x8, waiting for transfers between devices, shifted_2(): return lax.ppermute(value, axis, pairs)  144 us
    reduce_scatter x1, waiting for transfers between devices, on_device(): lax.psum_scatter(lax.dot_general(reordered, grad_projected, (((0,), (0,))...  87.9 us
    ppermute x7, starting transfers between devices, shifted(): return lax.ppermute(block, axis, route)  59.7 us
    unnamed x29, local copies, waits for them, and re-layouts  19.3 us
    ppermute x8, starting transfers between devices, shifted_2(): return lax.ppermute(value, axis, pairs)  14.7 us
  transfers between devices with their start and end apart: 18, of which 17 were waited for; matrix products, arithmetic and copies ran while one was open for 9% of the time, Pallas kernels for 0%

profile of v1, /device:TPU:0, one launch (start us, length us, event | category | flops | bytes accessed | tf_op | source)
XLA Modules:
  0.0 610.4 jit_solution(12476870145067675085)
XLA Ops:
  7.2 5.2 stack.2
  12.4 7.5 %all-to-all-start = ((bf16[32,128,1024]{2,1,0:T(8,128)(2,1)}), bf16[32,128,1024]{2,1,0:T(8,128)(2,1)}, u32[]{:S(2)}, u32[]{:S(2)}) async-start(bf16[32,128,1024]{2,1,0:T(8,128)(2,1)} %stack.2), calls=%async_computation | async-start | bytes 16777216 | tf_op jit(solution)/shard_map/all_to_all | solution.py:68
  19.9 1.9 copy.141
  21.9 4.3 copy.110
  26.1 2.3 reshape.246
  28.4 2.2 copy.139
  30.6 3.8 copy.102
  34.4 2.8 reshape.243
  37.3 2.5 copy.107
  39.7 2.3 copy.115
  42.0 2.3 copy.116
  45.5 159.1 %all-to-all-done = bf16[32,128,1024]{2,1,0:T(8,128)(2,1)} async-done(((bf16[32,128,1024]{2,1,0:T(8,128)(2,1)}), bf16[32,128,1024]{2,1,0:T(8,128)(2,1)}, u32[]{:S(2)}, u32[]{:S(2)}) %all-to-all-start) | async-done | bytes 8388640 | tf_op jit(solution)/shard_map/all_to_all | solution.py:68
  204.7 5.0 fusion.27
  217.8 2.1 fusion.41
  220.6 3.3 convolution_add_fusion.1
  225.6 68.0 %while.38 = (s32[]{:T(128)}, bf16[128,1024]{0,1:T(8,128)(2,1)S(1)}, bf16[8,128,1024]{1,2,0:T(8,128)(2,1)}, f32[4,2048,1]{1,0,2:T(4,128)S(1)}, f32[4,2048,1]{1,0,...) while((s32[]{:T(128)}, bf16[128,1024]{0,1:T(8,128)(2,1)S(1)}, ...), condition=%wide.region_7.8_spmd.clone, body=%wide.region_2.7_spmd.clone.sunk | while | flops 551063552 | bytes 61154760 | solution.py:155
  228.4 13.7 %collective-permute-start = (bf16[128,1024]{0,1:T(8,128)(2,1)S(1)}, bf16[128,1024]{0,1:T(8,128)(2,1)S(1)}, u32[]{:S(2)}, u32[]{:S(2)}) collective-permute-start(bf16[128,1024]{0,1:T(8,128)(2,1)S(1)} %get-tuple-element.850), channel_id=1, source_target_pairs={{0,1},{1,2},{2,3},{3,4},{4,5},{5,6},{6,7},{8,9},{9,10},{10,11},{11... | collective-permute-start | bytes 786440 | tf_op jit(solution)/shard_map/while/body/eval_jaxpr/ppermute | solution.py:13
  243.4 6.6 %collective-permute-start = (bf16[128,1024]{0,1:T(8,128)(2,1)S(1)}, bf16[128,1024]{0,1:T(8,128)(2,1)S(1)}, u32[]{:S(2)}, u32[]{:S(2)}) collective-permute-start(bf16[128,1024]{0,1:T(8,128)(2,1)S(1)} %get-tuple-element.850), channel_id=1, source_target_pairs={{0,1},{1,2},{2,3},{3,4},{4,5},{5,6},{6,7},{8,9},{9,10},{10,11},{11... | collective-permute-start | bytes 786440 | tf_op jit(solution)/shard_map/while/body/eval_jaxpr/ppermute | solution.py:13
  251.1 16.2 %collective-permute-start = (bf16[128,1024]{0,1:T(8,128)(2,1)S(1)}, bf16[128,1024]{0,1:T(8,128)(2,1)S(1)}, u32[]{:S(2)}, u32[]{:S(2)}) collective-permute-start(bf16[128,1024]{0,1:T(8,128)(2,1)S(1)} %get-tuple-element.850), channel_id=1, source_target_pairs={{0,1},{1,2},{2,3},{3,4},{4,5},{5,6},{6,7},{8,9},{9,10},{10,11},{11... | collective-permute-start | bytes 786440 | tf_op jit(solution)/shard_map/while/body/eval_jaxpr/ppermute | solution.py:13
  268.5 6.6 %collective-permute-start = (bf16[128,1024]{0,1:T(8,128)(2,1)S(1)}, bf16[128,1024]{0,1:T(8,128)(2,1)S(1)}, u32[]{:S(2)}, u32[]{:S(2)}) collective-permute-start(bf16[128,1024]{0,1:T(8,128)(2,1)S(1)} %get-tuple-element.850), channel_id=1, source_target_pairs={{0,1},{1,2},{2,3},{3,4},{4,5},{5,6},{6,7},{8,9},{9,10},{10,11},{11... | collective-permute-start | bytes 786440 | tf_op jit(solution)/shard_map/while/body/eval_jaxpr/ppermute | solution.py:13
  276.2 8.5 %collective-permute-start = (bf16[128,1024]{0,1:T(8,128)(2,1)S(1)}, bf16[128,1024]{0,1:T(8,128)(2,1)S(1)}, u32[]{:S(2)}, u32[]{:S(2)}) collective-permute-start(bf16[128,1024]{0,1:T(8,128)(2,1)S(1)} %get-tuple-element.850), channel_id=1, source_target_pairs={{0,1},{1,2},{2,3},{3,4},{4,5},{5,6},{6,7},{8,9},{9,10},{10,11},{11... | collective-permute-start | bytes 786440 | tf_op jit(solution)/shard_map/while/body/eval_jaxpr/ppermute | solution.py:13
  285.8 6.6 %collective-permute-start = (bf16[128,1024]{0,1:T(8,128)(2,1)S(1)}, bf16[128,1024]{0,1:T(8,128)(2,1)S(1)}, u32[]{:S(2)}, u32[]{:S(2)}) collective-permute-start(bf16[128,1024]{0,1:T(8,128)(2,1)S(1)} %get-tuple-element.850), channel_id=1, source_target_pairs={{0,1},{1,2},{2,3},{3,4},{4,5},{5,6},{6,7},{8,9},{9,10},{10,11},{11... | collective-permute-start | bytes 786440 | tf_op jit(solution)/shard_map/while/body/eval_jaxpr/ppermute | solution.py:13
  293.6 5.4 copy.108
  299.0 5.0 multiply_reduce_fusion
  304.0 2.2 broadcast.184
  306.2 170.9 %while.39 = (s32[]{:T(128)}, f32[128,1024]{0,1:T(8,128)S(1)}, f32[4,2048,128]{2,1,0:T(8,128)}, s32[]{:T(128)}, bf16[8,128,1024]{1,2,0:T(8,128)(2,1)}, /*index=5*...) while((s32[]{:T(128)}, f32[128,1024]{0,1:T(8,128)S(1)}, ...), condition=%wide.region_12.13_spmd.clone, body=%wide.region_9.12_spmd.clone.sunk | while | flops 1351823360 | bytes 85468640 | solution.py:215
  306.3 10.6 %conditional.7 = ((f32[128,1024]{0,1:T(8,128)S(1)}, f32[4,2048,128]{2,1,0:T(8,128)})) conditional(s32[]{:T(128)} %convert_element_type.142, (f32[128,1024]{0,1:T(8,128)S(1)}, f32[4,2048,128]{2,1,0:T(8,128)}) %tuple.112, (s32[]{:T(128)}, s32[]{:T(128)}, s32[2048]{0:T(1024)S(1)}, s32[128]{0:T(128)S(1)}, bf16[8,128,1024]{1,2,0:T(8,128)(2,1)}, ...), branch_computations={%region_10.10_spmd, %region_11.11_spmd.clone} | conditional | flops 1351428096 | bytes 81781416 | solution.py:211
  312.7 2.2 convolution_add_fusion
  314.9 1.9 copy-done.4
  316.9 14.3 %collective-permute-start.1 = (bf16[128,1024]{0,1:T(8,128)(2,1)S(1)}, bf16[128,1024]{0,1:T(8,128)(2,1)S(1)}, u32[]{:S(2)}, u32[]{:S(2)}) collective-permute-start(bf16[128,1024]{0,1:T(8,128)(2,1)S(1)} %convert_element_type.143), channel_id=1, source_target_pairs={{0,1},{1,2},{2,3},{3,4},{4,5},{5,6},{6,7},{7,0},{8,9},{9,10},{10,1... | collective-permute-start | bytes 786440 | tf_op jit(solution)/shard_map/while/body/eval_jaxpr/ppermute | solution.py:19
  331.2 38.8 %collective-permute-done.1 = bf16[128,1024]{0,1:T(8,128)(2,1)S(1)} collective-permute-done((bf16[128,1024]{0,1:T(8,128)(2,1)S(1)}, bf16[128,1024]{0,1:T(8,128)(2,1)S(1)}, u32[]{:S(2)}, u32[]{:S(2)}) %collective-permute-start.1) | collective-permute-done | bytes 262176 | tf_op jit(solution)/shard_map/while/body/eval_jaxpr/ppermute | solution.py:19
  370.2 13.8 %collective-permute-done.1 = bf16[128,1024]{0,1:T(8,128)(2,1)S(1)} collective-permute-done((bf16[128,1024]{0,1:T(8,128)(2,1)S(1)}, bf16[128,1024]{0,1:T(8,128)(2,1)S(1)}, u32[]{:S(2)}, u32[]{:S(2)}) %collective-permute-start.1) | collective-permute-done | bytes 262176 | tf_op jit(solution)/shard_map/while/body/eval_jaxpr/ppermute | solution.py:19
  384.3 13.8 %collective-permute-done.1 = bf16[128,1024]{0,1:T(8,128)(2,1)S(1)} collective-permute-done((bf16[128,1024]{0,1:T(8,128)(2,1)S(1)}, bf16[128,1024]{0,1:T(8,128)(2,1)S(1)}, u32[]{:S(2)}, u32[]{:S(2)}) %collective-permute-start.1) | collective-permute-done | bytes 262176 | tf_op jit(solution)/shard_map/while/body/eval_jaxpr/ppermute | solution.py:19
  398.4 13.8 %collective-permute-done.1 = bf16[128,1024]{0,1:T(8,128)(2,1)S(1)} collective-permute-done((bf16[128,1024]{0,1:T(8,128)(2,1)S(1)}, bf16[128,1024]{0,1:T(8,128)(2,1)S(1)}, u32[]{:S(2)}, u32[]{:S(2)}) %collective-permute-start.1) | collective-permute-done | bytes 262176 | tf_op jit(solution)/shard_map/while/body/eval_jaxpr/ppermute | solution.py:19
  412.5 14.8 %collective-permute-done.1 = bf16[128,1024]{0,1:T(8,128)(2,1)S(1)} collective-permute-done((bf16[128,1024]{0,1:T(8,128)(2,1)S(1)}, bf16[128,1024]{0,1:T(8,128)(2,1)S(1)}, u32[]{:S(2)}, u32[]{:S(2)}) %collective-permute-start.1) | collective-permute-done | bytes 262176 | tf_op jit(solution)/shard_map/while/body/eval_jaxpr/ppermute | solution.py:19
  427.6 16.3 %collective-permute-done.1 = bf16[128,1024]{0,1:T(8,128)(2,1)S(1)} collective-permute-done((bf16[128,1024]{0,1:T(8,128)(2,1)S(1)}, bf16[128,1024]{0,1:T(8,128)(2,1)S(1)}, u32[]{:S(2)}, u32[]{:S(2)}) %collective-permute-start.1) | collective-permute-done | bytes 262176 | tf_op jit(solution)/shard_map/while/body/eval_jaxpr/ppermute | solution.py:19
  444.2 16.3 %collective-permute-done.1 = bf16[128,1024]{0,1:T(8,128)(2,1)S(1)} collective-permute-done((bf16[128,1024]{0,1:T(8,128)(2,1)S(1)}, bf16[128,1024]{0,1:T(8,128)(2,1)S(1)}, u32[]{:S(2)}, u32[]{:S(2)}) %collective-permute-start.1) | collective-permute-done | bytes 262176 | tf_op jit(solution)/shard_map/while/body/eval_jaxpr/ppermute | solution.py:19
  460.8 16.3 %collective-permute-done.1 = bf16[128,1024]{0,1:T(8,128)(2,1)S(1)} collective-permute-done((bf16[128,1024]{0,1:T(8,128)(2,1)S(1)}, bf16[128,1024]{0,1:T(8,128)(2,1)S(1)}, u32[]{:S(2)}, u32[]{:S(2)}) %collective-permute-start.1) | collective-permute-done | bytes 262176 | tf_op jit(solution)/shard_map/while/body/eval_jaxpr/ppermute | solution.py:19
  478.4 5.6 convert_bitcast_fusion
  484.0 87.9 %reduce-scatter.5.cloned.1.call-done = bf16[512,1024]{0,1:T(8,128)(2,1)} async-done(((bf16[4096,1024]{0,1:T(8,128)(2,1)}), bf16[512,1024]{0,1:T(8,128)(2,1)}) %reduce-scatter.5.cloned.1.call-update) | async-done | bytes 1048592 | tf_op jit(solution)/shard_map/reduce_scatter | solution.py:231
  571.9 2.3 copy.131
  574.2 2.2 copy.140
  576.4 3.8 copy.109
  580.2 4.2 broadcast_in_dim_reshape.3
  584.3 2.8 multiply_convert_fusion
  587.1 2.7 copy.152
  589.9 4.2 convert_element_type.107
  594.0 7.4 %fusion.22 = bf16[1,128,4096]{2,1,0:T(8,128)(2,1)} fusion(bf16[4096,1024]{1,0:T(8,128)(2,1)} %bitcast.19, bf16[128,512]{0,1:T(8,128)(2,1)S(1)} %slice.61, bf16[128,512]{0,1:T(8,128)(2,1)S(1)} %bitcast.160), kind=kOutput, calls=%fused_computation.41 | convolution fusion | flops 1074790400 | bytes 9699328 | tf_op jit(solution)/shard_map/dot_general | solution.py:223
  (173 shorter events, 32.4 us)
Async XLA Ops:
  12.4 7.5 %copy-start.7 = (bf16[1,128,8192]{2,1,0:T(8,128)(2,1)S(1)}, bf16[1,128,8192]{2,1,0:T(8,128)(2,1)}, u32[]{:S(2)}) copy-start(bf16[1,128,8192]{2,1,0:T(8,128)(2,1)} %param.14) | copy-start | bytes 6291460
  12.4 192.2 %all-to-all-start = ((bf16[32,128,1024]{2,1,0:T(8,128)(2,1)}), bf16[32,128,1024]{2,1,0:T(8,128)(2,1)}, u32[]{:S(2)}, u32[]{:S(2)}) async-start(bf16[32,128,1024]{2,1,0:T(8,128)(2,1)} %stack.2), calls=%async_computation | async-start | bytes 16777216 | tf_op jit(solution)/shard_map/all_to_all | solution.py:68
  19.9 552.0 %reduce-scatter.5.cloned.1.call-start = ((), (), s32[]{:S(2)}) async-start(), calls=%async_computation.3 | async-start | bytes 9437184 | tf_op jit(solution)/shard_map/reduce_scatter | solution.py:231
  44.6 167.6 %copy-start.9 = (f32[128,64]{1,0:T(8,128)}, f32[128,64]{1,0:T(8,128)S(1)}, u32[]{:S(2)}) copy-start(f32[128,64]{1,0:T(8,128)S(1)} %get-tuple-element.707) | copy-start | bytes 98308
  44.7 167.6 %copy-start.11 = (f32[128,64]{1,0:T(8,128)}, f32[128,64]{1,0:T(8,128)S(1)}, u32[]{:S(2)}) copy-start(f32[128,64]{1,0:T(8,128)S(1)} %get-tuple-element.708) | copy-start | bytes 98308
  220.6 3.6 copy-start.8
  220.6 5.0 copy-start.13
  224.3 1.3 copy-start.5
  225.6 2.8 collective-permute-start
  228.4 14.9 %collective-permute-start = (bf16[128,1024]{0,1:T(8,128)(2,1)S(1)}, bf16[128,1024]{0,1:T(8,128)(2,1)S(1)}, u32[]{:S(2)}, u32[]{:S(2)}) collective-permute-start(bf16[128,1024]{0,1:T(8,128)(2,1)S(1)} %get-tuple-element.850), channel_id=1, source_target_pairs={{0,1},{1,2},{2,3},{3,4},{4,5},{5,6},{6,7},{8,9},{9,10},{10,11},{11... | collective-permute-start | bytes 786440 | tf_op jit(solution)/shard_map/while/body/eval_jaxpr/ppermute | solution.py:13
  243.4 7.7 %collective-permute-start = (bf16[128,1024]{0,1:T(8,128)(2,1)S(1)}, bf16[128,1024]{0,1:T(8,128)(2,1)S(1)}, u32[]{:S(2)}, u32[]{:S(2)}) collective-permute-start(bf16[128,1024]{0,1:T(8,128)(2,1)S(1)} %get-tuple-element.850), channel_id=1, source_target_pairs={{0,1},{1,2},{2,3},{3,4},{4,5},{5,6},{6,7},{8,9},{9,10},{10,11},{11... | collective-permute-start | bytes 786440 | tf_op jit(solution)/shard_map/while/body/eval_jaxpr/ppermute | solution.py:13
  251.1 17.3 %collective-permute-start = (bf16[128,1024]{0,1:T(8,128)(2,1)S(1)}, bf16[128,1024]{0,1:T(8,128)(2,1)S(1)}, u32[]{:S(2)}, u32[]{:S(2)}) collective-permute-start(bf16[128,1024]{0,1:T(8,128)(2,1)S(1)} %get-tuple-element.850), channel_id=1, source_target_pairs={{0,1},{1,2},{2,3},{3,4},{4,5},{5,6},{6,7},{8,9},{9,10},{10,11},{11... | collective-permute-start | bytes 786440 | tf_op jit(solution)/shard_map/while/body/eval_jaxpr/ppermute | solution.py:13
  268.5 7.7 %collective-permute-start = (bf16[128,1024]{0,1:T(8,128)(2,1)S(1)}, bf16[128,1024]{0,1:T(8,128)(2,1)S(1)}, u32[]{:S(2)}, u32[]{:S(2)}) collective-permute-start(bf16[128,1024]{0,1:T(8,128)(2,1)S(1)} %get-tuple-element.850), channel_id=1, source_target_pairs={{0,1},{1,2},{2,3},{3,4},{4,5},{5,6},{6,7},{8,9},{9,10},{10,11},{11... | collective-permute-start | bytes 786440 | tf_op jit(solution)/shard_map/while/body/eval_jaxpr/ppermute | solution.py:13
  276.2 9.6 %collective-permute-start = (bf16[128,1024]{0,1:T(8,128)(2,1)S(1)}, bf16[128,1024]{0,1:T(8,128)(2,1)S(1)}, u32[]{:S(2)}, u32[]{:S(2)}) collective-permute-start(bf16[128,1024]{0,1:T(8,128)(2,1)S(1)} %get-tuple-element.850), channel_id=1, source_target_pairs={{0,1},{1,2},{2,3},{3,4},{4,5},{5,6},{6,7},{8,9},{9,10},{10,11},{11... | collective-permute-start | bytes 786440 | tf_op jit(solution)/shard_map/while/body/eval_jaxpr/ppermute | solution.py:13
  285.8 7.7 %collective-permute-start = (bf16[128,1024]{0,1:T(8,128)(2,1)S(1)}, bf16[128,1024]{0,1:T(8,128)(2,1)S(1)}, u32[]{:S(2)}, u32[]{:S(2)}) collective-permute-start(bf16[128,1024]{0,1:T(8,128)(2,1)S(1)} %get-tuple-element.850), channel_id=1, source_target_pairs={{0,1},{1,2},{2,3},{3,4},{4,5},{5,6},{6,7},{8,9},{9,10},{10,11},{11... | collective-permute-start | bytes 786440 | tf_op jit(solution)/shard_map/while/body/eval_jaxpr/ppermute | solution.py:13
  306.2 171.3 %copy-start.10 = (f32[128,64]{1,0:T(8,128)S(1)}, f32[128,64]{1,0:T(8,128)}, u32[]{:S(2)}) copy-start(f32[128,64]{1,0:T(8,128)} %copy-done.9) | copy-start | bytes 98308
  306.2 171.3 %copy-start.12 = (f32[128,64]{1,0:T(8,128)S(1)}, f32[128,64]{1,0:T(8,128)}, u32[]{:S(2)}) copy-start(f32[128,64]{1,0:T(8,128)} %copy-done.11) | copy-start | bytes 98308
  307.3 1.7 copy-start
  310.5 2.2 copy-start.3
  314.9 1.9 copy-start.4
  316.9 53.1 %collective-permute-start.1 = (bf16[128,1024]{0,1:T(8,128)(2,1)S(1)}, bf16[128,1024]{0,1:T(8,128)(2,1)S(1)}, u32[]{:S(2)}, u32[]{:S(2)}) collective-permute-start(bf16[128,1024]{0,1:T(8,128)(2,1)S(1)} %convert_element_type.143), channel_id=1, source_target_pairs={{0,1},{1,2},{2,3},{3,4},{4,5},{5,6},{6,7},{7,0},{8,9},{9,10},{10,1... | collective-permute-start | bytes 786440 | tf_op jit(solution)/shard_map/while/body/eval_jaxpr/ppermute | solution.py:19
  370.2 13.9 %collective-permute-start.1 = (bf16[128,1024]{0,1:T(8,128)(2,1)S(1)}, bf16[128,1024]{0,1:T(8,128)(2,1)S(1)}, u32[]{:S(2)}, u32[]{:S(2)}) collective-permute-start(bf16[128,1024]{0,1:T(8,128)(2,1)S(1)} %convert_element_type.143), channel_id=1, source_target_pairs={{0,1},{1,2},{2,3},{3,4},{4,5},{5,6},{6,7},{7,0},{8,9},{9,10},{10,1... | collective-permute-start | bytes 786440 | tf_op jit(solution)/shard_map/while/body/eval_jaxpr/ppermute | solution.py:19
  384.3 13.9 %collective-permute-start.1 = (bf16[128,1024]{0,1:T(8,128)(2,1)S(1)}, bf16[128,1024]{0,1:T(8,128)(2,1)S(1)}, u32[]{:S(2)}, u32[]{:S(2)}) collective-permute-start(bf16[128,1024]{0,1:T(8,128)(2,1)S(1)} %convert_element_type.143), channel_id=1, source_target_pairs={{0,1},{1,2},{2,3},{3,4},{4,5},{5,6},{6,7},{7,0},{8,9},{9,10},{10,1... | collective-permute-start | bytes 786440 | tf_op jit(solution)/shard_map/while/body/eval_jaxpr/ppermute | solution.py:19
  398.4 13.9 %collective-permute-start.1 = (bf16[128,1024]{0,1:T(8,128)(2,1)S(1)}, bf16[128,1024]{0,1:T(8,128)(2,1)S(1)}, u32[]{:S(2)}, u32[]{:S(2)}) collective-permute-start(bf16[128,1024]{0,1:T(8,128)(2,1)S(1)} %convert_element_type.143), channel_id=1, source_target_pairs={{0,1},{1,2},{2,3},{3,4},{4,5},{5,6},{6,7},{7,0},{8,9},{9,10},{10,1... | collective-permute-start | bytes 786440 | tf_op jit(solution)/shard_map/while/body/eval_jaxpr/ppermute | solution.py:19
  412.5 14.9 %collective-permute-start.1 = (bf16[128,1024]{0,1:T(8,128)(2,1)S(1)}, bf16[128,1024]{0,1:T(8,128)(2,1)S(1)}, u32[]{:S(2)}, u32[]{:S(2)}) collective-permute-start(bf16[128,1024]{0,1:T(8,128)(2,1)S(1)} %convert_element_type.143), channel_id=1, source_target_pairs={{0,1},{1,2},{2,3},{3,4},{4,5},{5,6},{6,7},{7,0},{8,9},{9,10},{10,1... | collective-permute-start | bytes 786440 | tf_op jit(solution)/shard_map/while/body/eval_jaxpr/ppermute | solution.py:19
  427.6 16.4 %collective-permute-start.1 = (bf16[128,1024]{0,1:T(8,128)(2,1)S(1)}, bf16[128,1024]{0,1:T(8,128)(2,1)S(1)}, u32[]{:S(2)}, u32[]{:S(2)}) collective-permute-start(bf16[128,1024]{0,1:T(8,128)(2,1)S(1)} %convert_element_type.143), channel_id=1, source_target_pairs={{0,1},{1,2},{2,3},{3,4},{4,5},{5,6},{6,7},{7,0},{8,9},{9,10},{10,1... | collective-permute-start | bytes 786440 | tf_op jit(solution)/shard_map/while/body/eval_jaxpr/ppermute | solution.py:19
  444.1 16.4 %collective-permute-start.1 = (bf16[128,1024]{0,1:T(8,128)(2,1)S(1)}, bf16[128,1024]{0,1:T(8,128)(2,1)S(1)}, u32[]{:S(2)}, u32[]{:S(2)}) collective-permute-start(bf16[128,1024]{0,1:T(8,128)(2,1)S(1)} %convert_element_type.143), channel_id=1, source_target_pairs={{0,1},{1,2},{2,3},{3,4},{4,5},{5,6},{6,7},{7,0},{8,9},{9,10},{10,1... | collective-permute-start | bytes 786440 | tf_op jit(solution)/shard_map/while/body/eval_jaxpr/ppermute | solution.py:19
  460.7 16.4 %collective-permute-start.1 = (bf16[128,1024]{0,1:T(8,128)(2,1)S(1)}, bf16[128,1024]{0,1:T(8,128)(2,1)S(1)}, u32[]{:S(2)}, u32[]{:S(2)}) collective-permute-start(bf16[128,1024]{0,1:T(8,128)(2,1)S(1)} %convert_element_type.143), channel_id=1, source_target_pairs={{0,1},{1,2},{2,3},{3,4},{4,5},{5,6},{6,7},{7,0},{8,9},{9,10},{10,1... | collective-permute-start | bytes 786440 | tf_op jit(solution)/shard_map/while/body/eval_jaxpr/ppermute | solution.py:19
  477.1 1.2 copy-start.6
  483.9 117.5 %reduce-scatter.7.cloned.1.call-start = ((), (), s32[]{:S(2)}) async-start(), calls=%async_computation.4 | async-start | bytes 1310720
Sparse Core Ops, SparseCore 0:
  484.1 87.7 reduce-scatter.4
  574.8 26.4 reduce-scatter.6
